TPU v7x, 128 devices: a whole 4x4x4 slice. The times are simulated.
128 devices in a mesh: rep: 32 (over z, y, core), tensor: 4 (over x).
Axes of the slice: x: 4, y: 4, z: 4, core: 2. Of those that a mesh axis runs over, the one named last changes fastest.
Arguments:
- hidden_in: bfloat16 [2048, 4096], P('rep', 'tensor'), may hold values from -25 to 25
- query: bfloat16 [2048, 4096], P('rep', 'tensor'), may hold values from -6 to 6
- new_kv: bfloat16 [2048, 2, 512], P('rep', None, 'tensor'), may hold values from -8 to 8
- pool: bfloat16 [4096, 128, 2, 512], P('rep', None, None, 'tensor'), may hold values from -8 to 8
- page_table: int32 [2048, 2], P('rep'), may hold values from 0 to 127, as said below
- lengths: int32 [2048], replicated, may hold values from 1 to 256, 262144 in all
- dest: int32 [32], replicated, may hold values from 0 to 31, each once
- out_weight: bfloat16 [4096, 4096], P('tensor'), may hold values from -0.1875 to 0.1875
- norm_gain: float32 [4096], P('tensor'), may hold values from 0.1 to 1.9
- gate_up: bfloat16 [4096, 2, 11008], P('tensor', None, 'rep'), may hold values from -0.09375 to 0.09375
- down_weight: bfloat16 [11008, 4096], P('rep', 'tensor'), may hold values from -0.109375 to 0.109375
Outputs:
- layer_out: bfloat16 [2048, 4096], P('rep', 'tensor')
Inputs may be any that keep to these rules, and one draw needn't show every extreme that they name: `page_table`: within a group no two requests share a page.
All inputs are finite; a program needn't handle non-finite values.
Results may differ from a plain program's by a relative error of at most 0.03.
Values may be sent and summed in bfloat16 or wider, within the bound.
No kernel may reach another device: no remote copies, remote signals or barrier semaphores. Data moves between devices by JAX's collectives and lax.ppermute only.
A program may use at most 128 MiB of HBM per device.

v0:
```python
import jax
import jax.numpy as jnp
from jax import lax
from jax.sharding import PartitionSpec as P

D = 4096
HD = 128
EPSILON = 1e-05


def attend(queries, cache_block, new_pair, counts):
    row_count = cache_block.shape[0]
    cache_len = cache_block.shape[1]
    kv_width = cache_block.shape[3]
    kv_heads = kv_width // HD
    group_size = queries.shape[1] // kv_width
    query_heads = queries.reshape(row_count, kv_heads, group_size, HD)
    key_heads = cache_block[:, :, 0].reshape(row_count, cache_len, kv_heads, HD)
    value_heads = cache_block[:, :, 1].reshape(row_count, cache_len, kv_heads, HD)
    new_key = new_pair[:, 0].reshape(row_count, kv_heads, HD)
    new_value = new_pair[:, 1].reshape(row_count, kv_heads, HD)
    score_scale = HD ** (-0.5)
    scores = (
        jnp.einsum("nkgd,nlkd->nkgl", query_heads, key_heads, preferred_element_type=jnp.float32)
        * score_scale
    )
    own_score = (
        jnp.einsum("nkgd,nkd->nkg", query_heads, new_key, preferred_element_type=jnp.float32)
        * score_scale
    )
    in_range = (jnp.arange(cache_len, dtype=jnp.int32)[None, :] < counts[:, None])[:, None, None, :]
    masked = jnp.where(in_range, scores, -jnp.inf)
    peak_score = jnp.maximum(jnp.max(masked, axis=-1), own_score)
    weights = jnp.where(in_range, jnp.exp(scores - peak_score[..., None]), 0.0)
    own_weight = jnp.exp(own_score - peak_score)
    denominator = jnp.sum(weights, axis=-1) + own_weight
    weighted = jnp.einsum(
        "nkgl,nlkd->nkgd",
        weights.astype(jnp.bfloat16),
        value_heads,
        preferred_element_type=jnp.float32,
    )
    weighted = weighted + jnp.einsum(
        "nkg,nkd->nkgd",
        own_weight.astype(jnp.bfloat16),
        new_value,
        preferred_element_type=jnp.float32,
    )
    return (weighted / denominator[..., None]).astype(jnp.bfloat16).reshape(row_count, -1)


def local(
    hidden_in,
    query,
    new_kv,
    pool,
    page_table,
    lengths,
    dest,
    out_weight,
    norm_gain,
    gate_up,
    down_weight,
):
    rows_here = hidden_in.shape[0]
    group_count = lax.axis_size("rep")
    my_group = lax.axis_index("rep")
    group_ids = jnp.arange(group_count, dtype=jnp.int32)
    source = jnp.sum(jnp.where(dest == my_group, group_ids, 0))
    page_count = page_table.shape[1]
    page_len = pool.shape[1]
    kv_width = pool.shape[3]
    cache_rows = pool[page_table].reshape(rows_here, page_count * page_len, 2, kv_width)
    my_lengths = lax.dynamic_slice_in_dim(lengths, my_group * rows_here, rows_here)
    home_attn = attend(query, cache_rows, new_kv, my_lengths)
    every_attn, every_hidden = (
        lax.all_gather(home_attn[-1:], "rep", axis=0, tiled=True),
        lax.all_gather(hidden_in[-1:], "rep", axis=0, tiled=True),
    )
    attention = jnp.concatenate(
        [home_attn[:-1], lax.dynamic_slice_in_dim(every_attn, source, 1)], axis=0
    )
    served = jnp.concatenate(
        [hidden_in[:-1], lax.dynamic_slice_in_dim(every_hidden, source, 1)], axis=0
    )
    projected = jnp.dot(attention, out_weight, preferred_element_type=jnp.float32)
    head_total = lax.psum_scatter(
        projected.astype(jnp.bfloat16), "tensor", scatter_dimension=1, tiled=True
    ).astype(jnp.float32)
    residual = served.astype(jnp.float32) + head_total
    square_sum = lax.psum(jnp.sum(residual * residual, axis=1), "tensor")
    normed = (residual * lax.rsqrt(square_sum / D + EPSILON)[:, None] * norm_gain[None, :]).astype(
        jnp.bfloat16
    )
    unit_count = gate_up.shape[2]
    flat_weight = gate_up.reshape(gate_up.shape[0], 2 * unit_count)
    partial_units = jnp.dot(
        lax.all_gather(normed, "rep", axis=0, tiled=True),
        flat_weight,
        preferred_element_type=jnp.float32,
    )
    partial_units = partial_units.reshape(partial_units.shape[0], 2, unit_count)
    unit_total = lax.psum(partial_units.astype(jnp.bfloat16), "tensor").astype(jnp.float32)
    activated = (jax.nn.silu(unit_total[:, 0]) * unit_total[:, 1]).astype(jnp.bfloat16)
    mixed = lax.psum_scatter(
        jnp.dot(activated, down_weight, preferred_element_type=jnp.float32).astype(jnp.bfloat16),
        "rep",
        scatter_dimension=0,
        tiled=True,
    ).astype(jnp.float32)
    return (residual + mixed).astype(jnp.bfloat16)


def solution(mesh):
    return jax.shard_map(
        local,
        mesh=mesh,
        in_specs=(
            P("rep", "tensor"),
            P("rep", "tensor"),
            P("rep", None, "tensor"),
            P("rep", None, None, "tensor"),
            P("rep", None),
            P(),
            P(),
            P("tensor", None),
            P("tensor"),
            P("tensor", None, "rep"),
            P("rep", "tensor"),
        ),
        out_specs=P("rep", "tensor"),
        check_vma=False,
    )
```

profile of v0, /device:TPU:0, one launch (start us, length us, event | category | flops | bytes accessed | tf_op | source)
XLA Modules:
  0.0 336.0 jit_solution(7279921076718886438)
XLA Ops:
  6.5 0.8 compare_select_fusion
  7.3 0.1 copy.17
  7.4 0.1 reshape.104
  7.6 23.2 %gather_fusion = bf16[128,128,2,128]{3,2,1,0:T(2,128)(2,1)} fusion(bf16[128,128,2,128]{3,2,1,0:T(2,128)(2,1)} %param.14, s32[1024]{0:T(1024)S(1)} %pad_clamp_fusion), kind=kCustom, calls=%fused_computation | custom fusion | bytes 16777728 | tf_op jit(solution)/shard_map/gather | solution.py:73
  30.8 8.9 %copy.18 = bf16[128,128,2,128]{3,1,0,2:T(8,128)(2,1)} copy(bf16[128,128,2,128]{3,2,1,0:T(2,128)(2,1)} %gather_fusion) | data formatting | bytes 16777216 | tf_op jit(solution)/shard_map/gather | solution.py:73
  39.7 0.8 dynamic_slice.10
  40.4 0.1 iota_compare_fusion
  40.6 0.2 fusion.22
  40.8 3.5 %select_reduce_fusion = (f32[64,8]{1,0:T(8,128)S(1)}, f32[64,256,8]{1,2,0:T(8,128)S(1)}) fusion(pred[64,256]{1,0:T(8,128)(4,1)S(1)} %iota_compare_fusion, bf16[64,8,128]{2,1,0:T(8,128)(2,1)S(1)} %bitcast.79, bf16[64,256,2,128]{3,1,0,2:T(8,128)(2,1)} %bitcast.68), kind=kOutput, calls=%fused_computation.23 | convolution fusion | flops 33947136 | bytes 4868096 | tf_op jit(solution)/shard_map/nkgd,nlkd->nkgl/dot_general | solution.py:24
  44.3 0.3 bitcast_reduce_fusion
  44.6 2.9 fusion.15
  47.5 26.2 %all-gather.1 = bf16[32,1,1024]{2,1,0:T(2,128)(2,1)S(1)} all-gather(bf16[1,1,1024]{2,1,0:T(2,128)(2,1)S(1)} %reshape.115), channel_id=1, replica_groups=mesh['rep'=32,'tensor'=4] {'rep'}, dimensions={0}, use_global_device_ids=true | all-gather | bytes 67584 | tf_op jit(solution)/shard_map/all_gather | solution.py:77
  73.7 0.6 fusion.25
  76.4 5.8 %convolution_convert_fusion = bf16[64,4096]{1,0:T(8,128)(2,1)} fusion(bf16[1024,4096]{1,0:T(8,128)(2,1)} %param.18, bf16[1,1024]{1,0:T(2,128)(2,1)S(1)} %dynamic-slice_bitcast_fusion, bf16[63,1024]{1,0:T(8,128)(2,1)S(1)} %bitcast.73), kind=kOutput, calls=%fused_computation.1 | convolution fusion | flops 537395200 | bytes 9043968 | tf_op jit(solution)/shard_map/dot_general | solution.py:86
  82.2 0.0 reduce-scatter.3.cloned.1.call-update
  82.2 0.0 all-gather.4.cloned.1.call-start
  82.3 24.0 %all-gather = bf16[32,1,1024]{2,1,0:T(2,128)(2,1)S(1)} all-gather(bf16[1,1,1024]{2,1,0:T(2,128)(2,1)S(1)} %slice_bitcast_fusion.14), channel_id=1, replica_groups=mesh['rep'=32,'tensor'=4] {'rep'}, dimensions={0}, use_global_device_ids=true | all-gather | bytes 67584 | tf_op jit(solution)/shard_map/all_gather | solution.py:78
  106.3 1.1 multiply_reduce_fusion
  107.4 10.5 %psum.14 = f32[64]{0:T(128)S(1)} all-reduce(f32[64]{0:T(128)S(1)} %multiply_reduce_fusion), channel_id=1, replica_groups=mesh['rep'=32,'tensor'=4] {'tensor'}, use_global_device_ids=true, to_apply=%region_5.6 | all-reduce | flops 64 | bytes 512 | tf_op jit(solution)/shard_map/psum | solution.py:91
  117.9 1.7 multiply_convert_fusion
  119.6 0.0 all-gather.4.cloned.1.call-update
  119.6 0.0 all-reduce.2.cloned.1.call-start
  119.6 42.7 %all-gather.4.cloned.1.call-done = bf16[2048,1024]{1,0:T(8,128)(2,1)} async-done(((bf16[64,1024]{1,0:T(8,128)(2,1)}), bf16[2048,1024]{1,0:T(8,128)(2,1)}) %all-gather.4.cloned.1.call-update) | async-done | bytes 4194320 | tf_op jit(solution)/shard_map/all_gather | solution.py:98
  162.3 6.7 %fusion.4 = bf16[2048,2,344]{0,2,1:T(8,128)(2,1)} fusion(bf16[2048,1024]{1,0:T(8,128)(2,1)} %all-gather.4.cloned.1.call-done, bf16[1024,2,344]{0,2,1:T(8,128)(2,1)S(1)} %copy-done), kind=kOutput, calls=%fused_computation.9 | convolution fusion | flops 2887090176 | bytes 8421376 | tf_op jit(solution)/shard_map/dot_general | solution.py:97
  169.0 0.0 all-reduce.2.cloned.1.call-update
  169.0 0.2 reduce-scatter.5.cloned.1.call-start
  169.3 69.5 %all-reduce.2.cloned.1.call-done = bf16[2048,2,344]{0,2,1:T(8,128)(2,1)} async-done(((bf16[2048,2,344]{0,2,1:T(8,128)(2,1)}), bf16[2048,2,344]{0,2,1:T(8,128)(2,1)}) %all-reduce.2.cloned.1.call-update) | async-done | bytes 2818064 | tf_op jit(solution)/shard_map/psum | solution.py:103
  238.8 2.5 convert_element_type.50
  241.3 4.4 %convolution_convert_fusion.1 = bf16[2048,1024]{1,0:T(8,128)(2,1)} fusion(bf16[344,1024]{1,0:T(8,128)(2,1)S(1)} %copy-done.6, f32[2048,2,344]{0,2,1:T(8,128)S(1)} %convert_element_type.50), kind=kOutput, calls=%fused_computation.8 | convolution fusion | flops 1449164800 | bytes 10534912 | tf_op jit(solution)/shard_map/dot_general | solution.py:106
  245.8 0.0 reduce-scatter.5.cloned.1.call-update
  245.8 82.1 %reduce-scatter.5.cloned.1.call-done = bf16[64,1024]{1,0:T(8,128)(2,1)} async-done(((bf16[2048,1024]{1,0:T(8,128)(2,1)}), bf16[64,1024]{1,0:T(8,128)(2,1)}) %reduce-scatter.5.cloned.1.call-update) | async-done | bytes 131088 | tf_op jit(solution)/shard_map/reduce_scatter | solution.py:105
  327.9 1.6 add_convert_fusion
  (33 shorter events, 0.2 us)
Async XLA Ops:
  6.5 155.8 %copy-start = (bf16[1024,2,344]{0,2,1:T(8,128)(2,1)S(1)}, bf16[1024,2,344]{0,2,1:T(8,128)(2,1)}, u32[]{:S(2)}) copy-start(bf16[1024,2,344]{0,2,1:T(8,128)(2,1)} %param.20) | copy-start | bytes 4227076
  6.5 99.8 %reduce-scatter.3.cloned.1.call-start = ((), (), s32[]{:S(2)}) async-start(), calls=%async_computation.2 | async-start | bytes 655360 | tf_op jit(solution)/shard_map/reduce_scatter | solution.py:87
  30.8 9.7 %copy-start.3 = (bf16[64,1024]{1,0:T(8,128)(2,1)S(1)}, bf16[64,1024]{1,0:T(8,128)(2,1)}, u32[]{:S(2)}) copy-start(bf16[64,1024]{1,0:T(8,128)(2,1)} %param.12) | copy-start | bytes 393220
  30.8 9.8 %copy-start.4 = (bf16[64,2,128]{2,1,0:T(2,128)(2,1)S(1)}, bf16[64,2,128]{2,1,0:T(2,128)(2,1)}, u32[]{:S(2)}) copy-start(bf16[64,2,128]{2,1,0:T(2,128)(2,1)} %param.13) | copy-start | bytes 98308
  44.3 29.4 %copy-start.7 = (s32[32]{0:T(128)S(1)}, s32[32]{0:T(128)}, u32[]{:S(2)}) copy-start(s32[32]{0:T(128)} %param.17) | copy-start | bytes 388
  76.4 5.9 %copy-start.1 = (bf16[64,1024]{1,0:T(8,128)(2,1)S(1)}, bf16[64,1024]{1,0:T(8,128)(2,1)}, u32[]{:S(2)}) copy-start(bf16[64,1024]{1,0:T(8,128)(2,1)} %param.11) | copy-start | bytes 393220
  76.4 41.5 %copy-start.5 = (f32[1024]{0:T(1024)S(1)}, f32[1024]{0:T(1024)}, u32[]{:S(2)}) copy-start(f32[1024]{0:T(1024)} %param.19) | copy-start | bytes 12292
  82.2 80.1 %all-gather.4.cloned.1.call-start = ((), (), s32[]{:S(2)}) async-start(), calls=%async_computation.3 | async-start | bytes 4325376 | tf_op jit(solution)/shard_map/all_gather | solution.py:98
  119.6 119.2 %all-reduce.2.cloned.1.call-start = ((), (), s32[]{:S(2)}) async-start(), calls=%async_computation.4 | async-start | bytes 5636096 | tf_op jit(solution)/shard_map/psum | solution.py:103
  169.0 72.3 %copy-start.6 = (bf16[344,1024]{1,0:T(8,128)(2,1)S(1)}, bf16[344,1024]{1,0:T(8,128)(2,1)}, u32[]{:S(2)}) copy-start(bf16[344,1024]{1,0:T(8,128)(2,1)} %param.21) | copy-start | bytes 2113540
  169.0 158.8 %reduce-scatter.5.cloned.1.call-start = ((), (), s32[]{:S(2)}) async-start(), calls=%async_computation.5 | async-start | bytes 4325376 | tf_op jit(solution)/shard_map/reduce_scatter | solution.py:105
  245.8 82.1 %copy-start.2 = (bf16[64,1024]{1,0:T(8,128)(2,1)S(1)}, bf16[64,1024]{1,0:T(8,128)(2,1)}, u32[]{:S(2)}) copy-start(bf16[64,1024]{1,0:T(8,128)(2,1)} %reduce-scatter.3.cloned.1.call-done) | copy-start | bytes 393220
Sparse Core Ops, SparseCore 0:
  82.3 20.4 reduce-scatter.2
  119.7 42.5 all-gather.3
  169.1 69.5 all-reduce.1
  245.9 81.9 reduce-scatter.4
where the time goes:
time: 336 us
  waiting for transfers between devices  194 us (58%)
  blocking collectives  60.7 us (18%)
  local copies, waits for them, and re-layouts  33.2 us (10%)
  matrix products  23.4 us (7%)
  between operations  15.3 us (5%)
  other arithmetic  8.71 us (3%)
    reduce_scatter x1, waiting for transfers between devices, local(): lax.psum_scatter(jnp.dot(activated, down_weight, preferred_element_type=j...  82.1 us
    psum x1, waiting for transfers between devices, local(): lax.psum(partial_units.astype(jnp.bfloat16), 'tensor').astype(jnp.float32)  69.5 us
    all_gather x1, waiting for transfers between devices, local(): lax.all_gather(normed, 'rep', axis=0, tiled=True)  42.7 us
    gather x2, local copies, waits for them, and re-layouts, local(): pool[page_table].reshape(rows_here, page_count * page_len, 2, kv_width)  32.1 us
    all_gather x1, blocking collectives, local(): lax.all_gather(home_attn[-1:], 'rep', axis=0, tiled=True)  26.2 us
    all_gather x1, blocking collectives, local(): lax.all_gather(hidden_in[-1:], 'rep', axis=0, tiled=True)  24 us
    psum x1, blocking collectives, local(): square_sum = lax.psum(jnp.sum(residual * residual, axis=1), 'tensor')  10.5 us
  transfers between devices with their start and end apart: 4, of which 3 were waited for; matrix products, arithmetic and copies ran while one was open for 0% of the time, Pallas kernels for 0%

commit v1 on v0

--- a/solution.py
+++ b/solution.py
@@ -74,7 +74,9 @@
     my_lengths = lax.dynamic_slice_in_dim(lengths, my_group * rows_here, rows_here)
     home_attn = attend(query, cache_rows, new_kv, my_lengths)
     every_attn, every_hidden = (
-        lax.all_gather(home_attn[-1:], "rep", axis=0, tiled=True),
+        jnp.concatenate(
+            lax.all_to_all(jnp.stack([home_attn[-1:]] * lax.axis_size("rep")), "rep", 0, 0), axis=0
+        ),
         lax.all_gather(hidden_in[-1:], "rep", axis=0, tiled=True),
     )
     attention = jnp.concatenate(

time: 336 us -> 325 us (0.967)
  blocking collectives: 60.7 us -> 33.3 us
  starting transfers between devices: 0.31 us -> 8.76 us
  waiting for transfers between devices: 194 us -> 199 us
    all_gather x1 -> x0, blocking collectives: 26.2 us -> none  [local(): lax.all_gather(home_attn[-1:], 'rep', axis=0, tiled=True)]
    all_to_all x0 -> x1, starting transfers between devices: none -> 8.41 us  [local(): lax.all_to_all(jnp.stack([home_attn[-1:]] * lax.axis_size('rep')), 'rep',...]
    all_to_all x0 -> x1, waiting for transfers between devices: none -> 4.57 us  [local(): lax.all_to_all(jnp.stack([home_attn[-1:]] * lax.axis_size('rep')), 'rep',...]
  transfers between devices with their start and end apart: 4 -> 5, of which waited for: 3 -> 4; matrix products, arithmetic and copies ran while one was open for 0% -> 0% of each run, Pallas kernels for 0% -> 0%
where the time goes in v1:
time: 325 us; the launch traced here: 324 us
  waiting for transfers between devices  199 us (61%)
  local copies, waits for them, and re-layouts  34.5 us (11%)
  blocking collectives  33.3 us (10%)
  matrix products  23.4 us (7%)
  between operations  15.4 us (5%)
  other arithmetic  9.8 us (3%)
  starting transfers between devices  8.76 us (3%)
    reduce_scatter x1, waiting for transfers between devices, local(): lax.psum_scatter(jnp.dot(activated, down_weight, preferred_element_type=j...  82.1 us
    psum x1, waiting for transfers between devices, local(): lax.psum(partial_units.astype(jnp.bfloat16), 'tensor').astype(jnp.float32)  69.5 us
    all_gather x1, waiting for transfers between devices, local(): lax.all_gather(normed, 'rep', axis=0, tiled=True)  43 us
    gather x2, local copies, waits for them, and re-layouts, local(): pool[page_table].reshape(rows_here, page_count * page_len, 2, kv_width)  32.1 us
    all_gather x1, blocking collectives, local(): lax.all_gather(hidden_in[-1:], 'rep', axis=0, tiled=True)  22.8 us
    psum x1, blocking collectives, local(): square_sum = lax.psum(jnp.sum(residual * residual, axis=1), 'tensor')  10.5 us
    all_to_all x1, starting transfers between devices, local(): lax.all_to_all(jnp.stack([home_attn[-1:]] * lax.axis_size('rep')), 'rep',...  8.41 us
    dot_general x1, matrix products, local(): jnp.dot(lax.all_gather(normed, 'rep', axis=0, tiled=True), flat_weight, p...  6.65 us
  transfers between devices with their start and end apart: 5, of which 4 were waited for; matrix products, arithmetic and copies ran while one was open for 0% of the time, Pallas kernels for 0%

profile of v1, /device:TPU:0, one launch (start us, length us, event | category | flops | bytes accessed | tf_op | source)
XLA Modules:
  0.0 324.4 jit_solution(13798632474212014526)
XLA Ops:
  6.5 0.8 compare_select_fusion
  7.3 0.1 copy.17
  7.4 0.1 reshape.111
  7.6 23.2 %gather_fusion = bf16[128,128,2,128]{3,2,1,0:T(2,128)(2,1)} fusion(bf16[128,128,2,128]{3,2,1,0:T(2,128)(2,1)} %param.14, s32[1024]{0:T(1024)S(1)} %pad_clamp_fusion), kind=kCustom, calls=%fused_computation | custom fusion | bytes 16777728 | tf_op jit(solution)/shard_map/gather | solution.py:73
  30.8 8.9 %copy.18 = bf16[128,128,2,128]{3,1,0,2:T(8,128)(2,1)} copy(bf16[128,128,2,128]{3,2,1,0:T(2,128)(2,1)} %gather_fusion) | data formatting | bytes 16777216 | tf_op jit(solution)/shard_map/gather | solution.py:73
  39.7 0.8 dynamic_slice.12
  40.4 0.1 iota_compare_fusion
  40.6 0.2 fusion.22
  40.8 3.5 %select_reduce_fusion = (f32[64,8]{1,0:T(8,128)S(1)}, f32[64,256,8]{1,2,0:T(8,128)S(1)}) fusion(pred[64,256]{1,0:T(8,128)(4,1)S(1)} %iota_compare_fusion, bf16[64,8,128]{2,1,0:T(8,128)(2,1)S(1)} %bitcast.81, bf16[64,256,2,128]{3,1,0,2:T(8,128)(2,1)} %bitcast.70), kind=kOutput, calls=%fused_computation.23 | convolution fusion | flops 33947136 | bytes 4868096 | tf_op jit(solution)/shard_map/nkgd,nlkd->nkgl/dot_general | solution.py:24
  44.3 0.3 bitcast_reduce_fusion
  44.6 2.9 fusion.15
  47.5 0.1 stack.5
  47.6 0.5 broadcast.44
  48.1 1.0 reduce.5
  49.1 0.7 reshape.126
  49.8 8.4 %all-to-all-start = ((bf16[32,2,512]{2,1,0:T(2,128)(2,1)}), bf16[32,2,512]{2,1,0:T(2,128)(2,1)S(1)}, u32[]{:S(2)}, u32[]{:S(2)}) async-start(bf16[32,2,512]{2,1,0:T(2,128)(2,1)} %reshape.126), calls=%async_computation | async-start | bytes 131072 | tf_op jit(solution)/shard_map/all_to_all | solution.py:78
  58.3 0.7 fusion.25
  61.1 4.6 %all-to-all-done = bf16[32,2,512]{2,1,0:T(2,128)(2,1)S(1)} async-done(((bf16[32,2,512]{2,1,0:T(2,128)(2,1)}), bf16[32,2,512]{2,1,0:T(2,128)(2,1)S(1)}, u32[]{:S(2)}, u32[]{:S(2)}) %all-to-all-start) | async-done | bytes 65568 | tf_op jit(solution)/shard_map/all_to_all | solution.py:78
  65.7 0.1 reshape.127
  65.8 5.8 %convolution_convert_fusion = bf16[64,4096]{1,0:T(8,128)(2,1)} fusion(bf16[1024,4096]{1,0:T(8,128)(2,1)} %param.18, bf16[1,1024]{1,0:T(2,128)(2,1)S(1)} %dynamic-slice_bitcast_fusion.1, bf16[63,1024]{1,0:T(8,128)(2,1)S(1)} %bitcast.75), kind=kOutput, calls=%fused_computation.1 | convolution fusion | flops 537395200 | bytes 9043968 | tf_op jit(solution)/shard_map/dot_general | solution.py:88
  71.7 22.8 %all-gather = bf16[32,1,1024]{2,1,0:T(2,128)(2,1)S(1)} all-gather(bf16[1,1,1024]{2,1,0:T(2,128)(2,1)S(1)} %slice_bitcast_fusion.14), channel_id=1, replica_groups=mesh['rep'=32,'tensor'=4] {'rep'}, dimensions={0}, use_global_device_ids=true | all-gather | bytes 67584 | tf_op jit(solution)/shard_map/all_gather | solution.py:80
  94.4 1.1 multiply_reduce_fusion
  95.5 10.5 %psum.14 = f32[64]{0:T(128)S(1)} all-reduce(f32[64]{0:T(128)S(1)} %multiply_reduce_fusion), channel_id=1, replica_groups=mesh['rep'=32,'tensor'=4] {'tensor'}, use_global_device_ids=true, to_apply=%region_5.6 | all-reduce | flops 64 | bytes 512 | tf_op jit(solution)/shard_map/psum | solution.py:93
  106.0 1.7 multiply_convert_fusion
  107.7 43.0 %all-gather.3.cloned.1.call-done = bf16[2048,1024]{1,0:T(8,128)(2,1)} async-done(((bf16[64,1024]{1,0:T(8,128)(2,1)}), bf16[2048,1024]{1,0:T(8,128)(2,1)}) %all-gather.3.cloned.1.call-update) | async-done | bytes 4194320 | tf_op jit(solution)/shard_map/all_gather | solution.py:100
  150.7 6.6 %fusion.4 = bf16[2048,2,344]{0,2,1:T(8,128)(2,1)} fusion(bf16[2048,1024]{1,0:T(8,128)(2,1)} %all-gather.3.cloned.1.call-done, bf16[1024,2,344]{0,2,1:T(8,128)(2,1)S(1)} %copy-done), kind=kOutput, calls=%fused_computation.9 | convolution fusion | flops 2887090176 | bytes 8421376 | tf_op jit(solution)/shard_map/dot_general | solution.py:99
  157.4 0.2 reduce-scatter.5.cloned.1.call-start
  157.6 69.5 %all-reduce.2.cloned.1.call-done = bf16[2048,2,344]{0,2,1:T(8,128)(2,1)} async-done(((bf16[2048,2,344]{0,2,1:T(8,128)(2,1)}), bf16[2048,2,344]{0,2,1:T(8,128)(2,1)}) %all-reduce.2.cloned.1.call-update) | async-done | bytes 2818064 | tf_op jit(solution)/shard_map/psum | solution.py:105
  227.2 2.5 convert_element_type.50
  229.7 4.4 %convolution_convert_fusion.1 = bf16[2048,1024]{1,0:T(8,128)(2,1)} fusion(bf16[344,1024]{1,0:T(8,128)(2,1)S(1)} %copy-done.6, f32[2048,2,344]{0,2,1:T(8,128)S(1)} %convert_element_type.50), kind=kOutput, calls=%fused_computation.8 | convolution fusion | flops 1449164800 | bytes 10534912 | tf_op jit(solution)/shard_map/dot_general | solution.py:108
  234.2 82.1 %reduce-scatter.5.cloned.1.call-done = bf16[64,1024]{1,0:T(8,128)(2,1)} async-done(((bf16[2048,1024]{1,0:T(8,128)(2,1)}), bf16[64,1024]{1,0:T(8,128)(2,1)}) %reduce-scatter.5.cloned.1.call-update) | async-done | bytes 131088 | tf_op jit(solution)/shard_map/reduce_scatter | solution.py:107
  316.3 1.6 add_convert_fusion
  (38 shorter events, 0.4 us)
Async XLA Ops:
  6.5 144.2 %copy-start = (bf16[1024,2,344]{0,2,1:T(8,128)(2,1)S(1)}, bf16[1024,2,344]{0,2,1:T(8,128)(2,1)}, u32[]{:S(2)}) copy-start(bf16[1024,2,344]{0,2,1:T(8,128)(2,1)} %param.20) | copy-start | bytes 4227076
  30.8 9.7 %copy-start.3 = (bf16[64,1024]{1,0:T(8,128)(2,1)S(1)}, bf16[64,1024]{1,0:T(8,128)(2,1)}, u32[]{:S(2)}) copy-start(bf16[64,1024]{1,0:T(8,128)(2,1)} %param.12) | copy-start | bytes 393220
  30.8 9.8 %copy-start.4 = (bf16[64,2,128]{2,1,0:T(2,128)(2,1)S(1)}, bf16[64,2,128]{2,1,0:T(2,128)(2,1)}, u32[]{:S(2)}) copy-start(bf16[64,2,128]{2,1,0:T(2,128)(2,1)} %param.13) | copy-start | bytes 98308
  44.3 14.0 %copy-start.7 = (s32[32]{0:T(128)S(1)}, s32[32]{0:T(128)}, u32[]{:S(2)}) copy-start(s32[32]{0:T(128)} %param.17) | copy-start | bytes 388
  49.8 15.9 %all-to-all-start = ((bf16[32,2,512]{2,1,0:T(2,128)(2,1)}), bf16[32,2,512]{2,1,0:T(2,128)(2,1)S(1)}, u32[]{:S(2)}, u32[]{:S(2)}) async-start(bf16[32,2,512]{2,1,0:T(2,128)(2,1)} %reshape.126), calls=%async_computation | async-start | bytes 131072 | tf_op jit(solution)/shard_map/all_to_all | solution.py:78
  58.2 36.2 %reduce-scatter.3.cloned.1.call-start = ((), (), s32[]{:S(2)}) async-start(), calls=%async_computation.3 | async-start | bytes 655360 | tf_op jit(solution)/shard_map/reduce_scatter | solution.py:89
  65.8 5.9 %copy-start.1 = (bf16[64,1024]{1,0:T(8,128)(2,1)S(1)}, bf16[64,1024]{1,0:T(8,128)(2,1)}, u32[]{:S(2)}) copy-start(bf16[64,1024]{1,0:T(8,128)(2,1)} %param.11) | copy-start | bytes 393220
  65.8 40.2 %copy-start.5 = (f32[1024]{0:T(1024)S(1)}, f32[1024]{0:T(1024)}, u32[]{:S(2)}) copy-start(f32[1024]{0:T(1024)} %param.19) | copy-start | bytes 12292
  71.6 79.1 %all-gather.3.cloned.1.call-start = ((), (), s32[]{:S(2)}) async-start(), calls=%async_computation.4 | async-start | bytes 4325376 | tf_op jit(solution)/shard_map/all_gather | solution.py:100
  107.7 119.5 %all-reduce.2.cloned.1.call-start = ((), (), s32[]{:S(2)}) async-start(), calls=%async_computation.5 | async-start | bytes 5636096 | tf_op jit(solution)/shard_map/psum | solution.py:105
  157.4 72.3 %copy-start.6 = (bf16[344,1024]{1,0:T(8,128)(2,1)S(1)}, bf16[344,1024]{1,0:T(8,128)(2,1)}, u32[]{:S(2)}) copy-start(bf16[344,1024]{1,0:T(8,128)(2,1)} %param.21) | copy-start | bytes 2113540
  157.4 158.9 %reduce-scatter.5.cloned.1.call-start = ((), (), s32[]{:S(2)}) async-start(), calls=%async_computation.6 | async-start | bytes 4325376 | tf_op jit(solution)/shard_map/reduce_scatter | solution.py:107
  234.2 82.1 %copy-start.2 = (bf16[64,1024]{1,0:T(8,128)(2,1)S(1)}, bf16[64,1024]{1,0:T(8,128)(2,1)}, u32[]{:S(2)}) copy-start(bf16[64,1024]{1,0:T(8,128)(2,1)} %reduce-scatter.3.cloned.1.call-done) | copy-start | bytes 393220
Sparse Core Ops, SparseCore 0:
  71.7 19.0 reduce-scatter.2
  107.8 42.8 all-gather.2
  157.5 69.6 all-reduce.1
  234.3 81.9 reduce-scatter.4
